TPU v7x, 256 devices: a whole 4x4x8 slice. The times are simulated.
256 devices in a mesh: grp: 32 (over z_lo, x, core), shard: 8 (over z_hi, y).
Axes of the slice: x: 4, y: 4, z: 8 (z_hi: 2, z_lo: 4; z = z_hi * 4 + z_lo), core: 2. Of those that a mesh axis runs over, the one named last changes fastest.
Arguments:
- tokens: bfloat16 [16384, 2560], P(('grp', 'shard')), may hold values from -0.125 to 0.125
- target: bfloat16 [16384, 13824], P('grp', 'shard'), may hold values from -6 to 6
- post_mean: float32 [2560, 13824], P('grp', 'shard'), may hold values from -5 to 5
- post_hess: float32 [2560, 13824], P('grp', 'shard'), may hold values from 0.05 to 0.5
- weight_noise: bfloat16 [32, 2560, 13824], P(None, 'grp', 'shard'), may hold values from -6 to 6
Outputs:
- new_mean: float32 [2560, 13824], P('grp', 'shard')
- new_hess: float32 [2560, 13824], P('grp', 'shard')
All inputs are finite; a program needn't handle non-finite values.
Results may differ from a plain program's by a relative error of at most 0.0018.
Values may be sent and summed in bfloat16 or wider, within the bound.
A program may use at most 192 MiB of HBM per device.

v0:
```python
import jax
import jax.numpy as jnp
from jax import lax
from jax.sharding import PartitionSpec as P

sample_size = 50.0
weight_decay = 0.02
hess_decay = 0.95
learn_rate = 0.3


def contract_rows(left, right):
    return lax.dot_general(
        left, right, (((0,), (0,)), ((), ())), preferred_element_type=jnp.float32
    )


def local(tokens, target, post_mean, post_hess, weight_noise):
    groups = weight_noise.shape[0]
    post_std = lax.rsqrt(sample_size * (post_hess + weight_decay))
    noise_vals = weight_noise.astype(jnp.float32)
    samples = (post_mean[None] + post_std[None] * noise_vals).astype(jnp.bfloat16)
    group_x = lax.all_gather(tokens, "shard", axis=0, tiled=True)
    output = jnp.dot(
        group_x,
        lax.all_to_all(samples, "grp", split_axis=0, concat_axis=1, tiled=True)[0],
        preferred_element_type=jnp.float32,
    )
    residual = (output - target.astype(jnp.float32)).astype(jnp.bfloat16)
    gradient = contract_rows(group_x, residual).astype(jnp.bfloat16)
    group_grads = lax.all_to_all(gradient[None], "grp", split_axis=1, concat_axis=0, tiled=True)
    group_grads = group_grads.astype(jnp.float32)
    mean_grad = jnp.sum(group_grads, axis=0) / groups
    hess_est = jnp.sum(group_grads * noise_vals, axis=0) / groups / post_std
    keep_rate = 1.0 - hess_decay
    gap = post_hess - hess_est
    new_hess = (
        hess_decay * post_hess
        + keep_rate * hess_est
        + 0.5 * keep_rate * keep_rate * gap * gap / (post_hess + weight_decay)
    )
    new_mean = post_mean - learn_rate * (mean_grad + weight_decay * post_mean) / (
        new_hess + weight_decay
    )
    return (new_mean, new_hess)


def solution(mesh):
    return jax.shard_map(
        local,
        mesh=mesh,
        in_specs=(
            P(("grp", "shard"), None),
            P("grp", "shard"),
            P("grp", "shard"),
            P("grp", "shard"),
            P(None, "grp", "shard"),
        ),
        out_specs=(P("grp", "shard"), P("grp", "shard")),
        check_vma=False,
    )
```

profile of v0, /device:TPU:1, one launch (start us, length us, event | category | flops | bytes accessed | tf_op | source)
XLA Modules:
  0.0 707.4 jit_solution(3777936069902256427)
XLA Ops:
  7.2 1.1 multiply_rsqrt_fusion
  8.3 9.5 %fusion.1 = bf16[32,80,1728]{2,1,0:T(8,128)(2,1)} fusion(bf16[32,80,1728]{2,1,0:T(8,128)(2,1)} %param.9, f32[80,1728]{1,0:T(8,128)S(1)} %multiply_rsqrt_fusion, f32[80,1728]{1,0:T(8,128)} %param.7), kind=kLoop, calls=%fused_computation.4 | loop fusion | flops 17694720 | bytes 18800640 | tf_op jit(solution)/shard_map/convert_element_type | solution.py:22
  17.8 0.0 copy-start.2
  17.8 10.2 %all-to-all-start = ((bf16[32,80,1728]{2,1,0:T(8,128)(2,1)}), bf16[32,80,1728]{2,1,0:T(8,128)(2,1)}, u32[]{:S(2)}, u32[]{:S(2)}) async-start(bf16[32,80,1728]{2,1,0:T(8,128)(2,1)} %fusion.1), calls=%async_computation | async-start | bytes 18350080 | tf_op jit(solution)/shard_map/all_to_all | solution.py:26
  28.0 0.2 all-gather.2.cloned.1.call-start
  28.2 0.5 all-gather.2.cloned.1.call-update
  28.7 108.1 %all-gather.2.cloned.1.call-done = bf16[512,2560]{1,0:T(8,128)(2,1)} async-done(((bf16[64,2560]{1,0:T(8,128)(2,1)}), bf16[512,2560]{1,0:T(8,128)(2,1)}) %all-gather.2.cloned.1.call-update) | async-done | bytes 2621456 | tf_op jit(solution)/shard_map/all_gather | solution.py:23
  136.9 129.7 %all-to-all-done = bf16[32,80,1728]{2,1,0:T(8,128)(2,1)} async-done(((bf16[32,80,1728]{2,1,0:T(8,128)(2,1)}), bf16[32,80,1728]{2,1,0:T(8,128)(2,1)}, u32[]{:S(2)}, u32[]{:S(2)}) %all-to-all-start) | async-done | bytes 8847392 | tf_op jit(solution)/shard_map/all_to_all | solution.py:26
  266.5 0.0 copy-done.2
  266.5 17.0 %fusion.3 = bf16[1,2560,1728]{1,2,0:T(8,128)(2,1)} fusion(bf16[512,2560]{1,0:T(8,128)(2,1)} %all-gather.2.cloned.1.call-done, bf16[512,1728]{0,1:T(8,128)(2,1)S(1)} %copy-done.2, bf16[2560,1728]{1,0:T(8,128)(2,1)} %bitcast), kind=kOutput, calls=%fused_computation.7 | convolution fusion | flops 9066774528 | bytes 22085632 | tf_op jit(solution)/shard_map/dot_general | solution.py:13
  283.6 37.2 %copy.9 = bf16[1,2560,1728]{2,0,1:T(2,128)(2,1)} copy(bf16[1,2560,1728]{1,2,0:T(8,128)(2,1)} %fusion.3) | data formatting | bytes 17694720 | tf_op jit(solution)/shard_map/broadcast_in_dim | solution.py:31
  320.7 0.5 broadcast.21
  321.2 101.7 %reduce = bf16[2560,1728]{1,0:T(8,128)(2,1)} reduce(bf16[2560,1,1728]{2,1,0:T(2,128)(2,1)} %bitcast.18, bf16[]{:T(256)} %broadcast.21), dimensions={1}, to_apply=%bitcast.13.reduce_sub_computation | reduce | bytes 17694722
  422.9 24.1 %reshape.16 = bf16[32,2,69120]{2,1,0:T(2,128)(2,1)} reshape(bf16[2560,1728]{1,0:T(8,128)(2,1)} %reduce) | data formatting | bytes 17694720
  447.0 200.5 %all_to_all.8 = bf16[32,2,69120]{2,1,0:T(2,128)(2,1)} all-to-all(bf16[32,2,69120]{2,1,0:T(2,128)(2,1)} %reshape.16), channel_id=1, replica_groups=mesh['grp'=32,'shard'=8] {'grp'}, dimensions={0} | all-to-all | bytes 17694720 | tf_op jit(solution)/shard_map/all_to_all | solution.py:31
  647.5 27.7 %reshape.17 = bf16[2560,1,1728]{2,1,0:T(2,128)(2,1)} reshape(bf16[32,2,69120]{2,1,0:T(2,128)(2,1)} %all_to_all.8) | data formatting | bytes 17694720
  675.3 14.1 %copy.10 = bf16[1,2560,1728]{2,1,0:T(8,128)(2,1)} copy(bf16[1,2560,1728]{2,0,1:T(2,128)(2,1)} %bitcast.19) | data formatting | bytes 17694720 | tf_op jit(solution)/shard_map/all_to_all | solution.py:31
  689.4 0.0 copy-start
  689.4 0.0 copy-start.1
  689.4 9.7 %convert_reduce_fusion = (f32[80,1728]{1,0:T(8,128)S(1)}, f32[80,1728]{1,0:T(8,128)S(1)}) fusion(bf16[32,80,1728]{2,1,0:T(8,128)(2,1)} %bitcast.20, bf16[32,80,1728]{2,1,0:T(8,128)(2,1)} %param.9), kind=kLoop, calls=%fused_computation.1 | loop fusion | flops 21841920 | bytes 18800640 | tf_op jit(solution)/shard_map/reduce_sum | solution.py:33
  699.1 0.0 copy-done
  699.1 0.0 copy-done.1
  699.1 1.4 divide_subtract_fusion
Async XLA Ops:
  17.8 248.8 %copy-start.2 = (bf16[512,1728]{0,1:T(8,128)(2,1)S(1)}, bf16[512,1728]{0,1:T(8,128)(2,1)}, u32[]{:S(2)}) copy-start(bf16[512,1728]{0,1:T(8,128)(2,1)} %param.6) | copy-start | bytes 5308420
  17.8 248.8 %all-to-all-start = ((bf16[32,80,1728]{2,1,0:T(8,128)(2,1)}), bf16[32,80,1728]{2,1,0:T(8,128)(2,1)}, u32[]{:S(2)}, u32[]{:S(2)}) async-start(bf16[32,80,1728]{2,1,0:T(8,128)(2,1)} %fusion.1), calls=%async_computation | async-start | bytes 18350080 | tf_op jit(solution)/shard_map/all_to_all | solution.py:26
  28.0 108.9 %all-gather.2.cloned.1.call-start = ((), (), s32[]{:S(2)}) async-start(), calls=%async_computation.2 | async-start | bytes 2949120 | tf_op jit(solution)/shard_map/all_gather | solution.py:23
  689.4 9.7 %copy-start = (f32[80,1728]{1,0:T(8,128)S(1)}, f32[80,1728]{1,0:T(8,128)}, u32[]{:S(2)}) copy-start(f32[80,1728]{1,0:T(8,128)} %param.7) | copy-start | bytes 1658884
  689.4 9.8 %copy-start.1 = (f32[80,1728]{1,0:T(8,128)S(1)}, f32[80,1728]{1,0:T(8,128)}, u32[]{:S(2)}) copy-start(f32[80,1728]{1,0:T(8,128)} %param.8) | copy-start | bytes 1658884
Sparse Core Ops, SparseCore 0:
  31.4 105.4 all-gather.1
where the time goes:
time: 710 us; the launch traced here: 707 us
  waiting for transfers between devices  238 us (34%)
  blocking collectives  201 us (28%)
  other arithmetic  123 us (17%)
  local copies, waits for them, and re-layouts  104 us (15%)
  matrix products  17 us (2%)
  between operations  14.1 us (2%)
  starting transfers between devices  10.4 us (1%)
    all_to_all x1, blocking collectives, local(): lax.all_to_all(gradient[None], 'grp', split_axis=1, concat_axis=0, tiled=...  201 us
    all_to_all x1, waiting for transfers between devices, local(): lax.all_to_all(samples, 'grp', split_axis=0, concat_axis=1, tiled=True)[0]  130 us
    all_gather x1, waiting for transfers between devices, local(): group_x = lax.all_gather(tokens, 'shard', axis=0, tiled=True)  108 us
    unnamed x1, other arithmetic  102 us
    unnamed x9, local copies, waits for them, and re-layouts  52.4 us
    broadcast_in_dim x1, local copies, waits for them, and re-layouts, local(): gradient[None]  37.2 us
    dot_general x1, matrix products, contract_rows(): lax.dot_general(left, right, (((0,), (0,)), ((), ())), preferred_element_...  17 us
  transfers between devices with their start and end apart: 2, of which 2 were waited for; matrix products, arithmetic and copies ran while one was open for 0% of the time, Pallas kernels for 0%

commit v1 on v0

--- a/solution.py
+++ b/solution.py
@@ -20,7 +20,9 @@
     post_std = lax.rsqrt(sample_size * (post_hess + weight_decay))
     noise_vals = weight_noise.astype(jnp.float32)
     samples = (post_mean[None] + post_std[None] * noise_vals).astype(jnp.bfloat16)
-    group_x = lax.all_gather(tokens, "shard", axis=0, tiled=True)
+    group_x = jnp.concatenate(
+        lax.all_to_all(jnp.stack([tokens] * lax.axis_size("shard")), "shard", 0, 0), axis=0
+    )
     output = jnp.dot(
         group_x,
         lax.all_to_all(samples, "grp", split_axis=0, concat_axis=1, tiled=True)[0],

time: 710 us -> 718 us (1.011)
  blocking collectives: 201 us -> 428 us
  waiting for transfers between devices: 238 us -> 30.3 us
  between operations: 14.1 us -> 0.66 us
    all_to_all x0 -> x1, blocking collectives: none -> 228 us  [local(): lax.all_to_all(samples, 'grp', split_axis=0, concat_axis=1, tiled=True)[0]]
    all_gather x1 -> x0, waiting for transfers between devices: 108 us -> none  [local(): group_x = lax.all_gather(tokens, 'shard', axis=0, tiled=True)]
    all_to_all x1, waiting for transfers between devices: 130 us -> 30.3 us  [local(): lax.all_to_all(jnp.stack([tokens] * lax.axis_size('shard')), 'shard', 0, 0)]
    unnamed x9 -> x7, local copies, waits for them, and re-layouts: 52.4 us -> 52.4 us
  transfers between devices with their start and end apart: 2 -> 1, of which waited for: 2 -> 1; matrix products, arithmetic and copies ran while one was open for 0% -> 2% of each run, Pallas kernels for 0% -> 0%
where the time goes in v1:
time: 718 us; the launch traced here: 716 us
  blocking collectives  428 us (60%)
  other arithmetic  124 us (17%)
  local copies, waits for them, and re-layouts  106 us (15%)
  waiting for transfers between devices  30.3 us (4%)
  matrix products  14.5 us (2%)
  starting transfers between devices  11.6 us (2%)
    all_to_all x1, blocking collectives, local(): lax.all_to_all(samples, 'grp', split_axis=0, concat_axis=1, tiled=True)[0]  228 us
    all_to_all x1, blocking collectives, local(): lax.all_to_all(gradient[None], 'grp', split_axis=1, concat_axis=0, tiled=...  200 us
    unnamed x1, other arithmetic  102 us
    unnamed x7, local copies, waits for them, and re-layouts  52.4 us
    broadcast_in_dim x1, local copies, waits for them, and re-layouts, local(): gradient[None]  37.2 us
    all_to_all x1, waiting for transfers between devices, local(): lax.all_to_all(jnp.stack([tokens] * lax.axis_size('shard')), 'shard', 0, 0)  30.3 us
    dot_general x1, matrix products, contract_rows(): lax.dot_general(left, right, (((0,), (0,)), ((), ())), preferred_element_...  14.5 us
  transfers between devices with their start and end apart: 1, of which 1 were waited for; matrix products, arithmetic and copies ran while one was open for 2% of the time, Pallas kernels for 0%

profile of v1, /device:TPU:1, one launch (start us, length us, event | category | flops | bytes accessed | tf_op | source)
XLA Modules:
  0.0 715.8 jit_solution(14909158271878799778)
XLA Ops:
  0.6 0.0 copy-start
  0.6 2.7 stack.2
  3.4 11.6 %all-to-all-start.1 = ((bf16[8,64,2560]{2,1,0:T(8,128)(2,1)}), bf16[8,64,2560]{2,1,0:T(8,128)(2,1)S(1)}, u32[]{:S(2)}, u32[]{:S(2)}) async-start(bf16[8,64,2560]{2,1,0:T(8,128)(2,1)} %stack.2), calls=%async_computation.1 | async-start | bytes 5242880 | tf_op jit(solution)/shard_map/all_to_all | solution.py:24
  15.0 1.9 multiply_rsqrt_fusion
  16.9 0.0 copy-done
  17.0 9.4 %fusion.1 = bf16[32,80,1728]{2,1,0:T(8,128)(2,1)} fusion(bf16[32,80,1728]{2,1,0:T(8,128)(2,1)} %param.9, f32[80,1728]{1,0:T(8,128)} %multiply_rsqrt_fusion, f32[80,1728]{1,0:T(8,128)S(1)} %copy-done), kind=kLoop, calls=%fused_computation.4 | loop fusion | flops 17694720 | bytes 18800640 | tf_op jit(solution)/shard_map/convert_element_type | solution.py:22
  26.4 30.3 %all-to-all-done.1 = bf16[8,64,2560]{2,1,0:T(8,128)(2,1)S(1)} async-done(((bf16[8,64,2560]{2,1,0:T(8,128)(2,1)}), bf16[8,64,2560]{2,1,0:T(8,128)(2,1)S(1)}, u32[]{:S(2)}, u32[]{:S(2)}) %all-to-all-start.1) | async-done | bytes 2621472 | tf_op jit(solution)/shard_map/all_to_all | solution.py:24
  56.7 228.4 %all_to_all.23 = bf16[32,80,1728]{2,1,0:T(8,128)(2,1)} all-to-all(bf16[32,80,1728]{2,1,0:T(8,128)(2,1)} %fusion.1), channel_id=1, replica_groups=mesh['grp'=32,'shard'=8] {'grp'}, dimensions={0} | all-to-all | bytes 17694720 | tf_op jit(solution)/shard_map/all_to_all | solution.py:28
  285.1 14.5 %fusion.3 = bf16[1,2560,1728]{1,2,0:T(8,128)(2,1)} fusion(bf16[512,2560]{1,0:T(8,128)(2,1)S(1)} %bitcast.23, bf16[512,1728]{0,1:T(8,128)(2,1)} %param.6, bf16[2560,1728]{1,0:T(8,128)(2,1)} %bitcast.22), kind=kOutput, calls=%fused_computation.7 | convolution fusion | flops 9066774528 | bytes 22085632 | tf_op jit(solution)/shard_map/dot_general | solution.py:13
  299.7 37.2 %copy.9 = bf16[1,2560,1728]{2,0,1:T(2,128)(2,1)} copy(bf16[1,2560,1728]{1,2,0:T(8,128)(2,1)} %fusion.3) | data formatting | bytes 17694720 | tf_op jit(solution)/shard_map/broadcast_in_dim | solution.py:33
  336.9 0.5 broadcast.23
  337.5 101.7 %reduce = bf16[2560,1728]{1,0:T(8,128)(2,1)} reduce(bf16[2560,1,1728]{2,1,0:T(2,128)(2,1)} %bitcast.19, bf16[]{:T(256)} %broadcast.23), dimensions={1}, to_apply=%bitcast.14.reduce_sub_computation | reduce | bytes 17694722
  439.1 24.1 %reshape.22 = bf16[32,2,69120]{2,1,0:T(2,128)(2,1)} reshape(bf16[2560,1728]{1,0:T(8,128)(2,1)} %reduce) | data formatting | bytes 17694720
  463.2 199.5 %all_to_all.24 = bf16[32,2,69120]{2,1,0:T(2,128)(2,1)} all-to-all(bf16[32,2,69120]{2,1,0:T(2,128)(2,1)} %reshape.22), channel_id=1, replica_groups=mesh['grp'=32,'shard'=8] {'grp'}, dimensions={0} | all-to-all | bytes 17694720 | tf_op jit(solution)/shard_map/all_to_all | solution.py:33
  662.8 27.8 %reshape.23 = bf16[2560,1,1728]{2,1,0:T(2,128)(2,1)} reshape(bf16[32,2,69120]{2,1,0:T(2,128)(2,1)} %all_to_all.24) | data formatting | bytes 17694720
  690.6 14.1 %copy.10 = bf16[1,2560,1728]{2,1,0:T(8,128)(2,1)} copy(bf16[1,2560,1728]{2,0,1:T(2,128)(2,1)} %bitcast.20) | data formatting | bytes 17694720 | tf_op jit(solution)/shard_map/all_to_all | solution.py:33
  704.6 0.0 copy-start.1
  704.6 9.7 %convert_reduce_fusion = (f32[80,1728]{1,0:T(8,128)S(1)}, f32[80,1728]{1,0:T(8,128)S(1)}) fusion(bf16[32,80,1728]{2,1,0:T(8,128)(2,1)} %bitcast.21, bf16[32,80,1728]{2,1,0:T(8,128)(2,1)} %param.9), kind=kLoop, calls=%fused_computation.1 | loop fusion | flops 21841920 | bytes 18800640 | tf_op jit(solution)/shard_map/reduce_sum | solution.py:35
  714.3 0.0 copy-done.1
  714.4 1.4 divide_subtract_fusion
Async XLA Ops:
  0.6 16.3 %copy-start = (f32[80,1728]{1,0:T(8,128)S(1)}, f32[80,1728]{1,0:T(8,128)}, u32[]{:S(2)}) copy-start(f32[80,1728]{1,0:T(8,128)} %param.7) | copy-start | bytes 1658884
  3.4 53.4 %all-to-all-start.1 = ((bf16[8,64,2560]{2,1,0:T(8,128)(2,1)}), bf16[8,64,2560]{2,1,0:T(8,128)(2,1)S(1)}, u32[]{:S(2)}, u32[]{:S(2)}) async-start(bf16[8,64,2560]{2,1,0:T(8,128)(2,1)} %stack.2), calls=%async_computation.1 | async-start | bytes 5242880 | tf_op jit(solution)/shard_map/all_to_all | solution.py:24
  704.6 9.7 %copy-start.1 = (f32[80,1728]{1,0:T(8,128)S(1)}, f32[80,1728]{1,0:T(8,128)}, u32[]{:S(2)}) copy-start(f32[80,1728]{1,0:T(8,128)} %param.8) | copy-start | bytes 1658884

commit v2 on v0

--- a/solution.py
+++ b/solution.py
@@ -28,7 +28,12 @@
     )
     residual = (output - target.astype(jnp.float32)).astype(jnp.bfloat16)
     gradient = contract_rows(group_x, residual).astype(jnp.bfloat16)
-    group_grads = lax.all_to_all(gradient[None], "grp", split_axis=1, concat_axis=0, tiled=True)
+    group_grads = jnp.concatenate(
+        lax.all_to_all(
+            jnp.stack(jnp.split(gradient[None], lax.axis_size("grp"), axis=1)), "grp", 0, 0
+        ),
+        axis=0,
+    )
     group_grads = group_grads.astype(jnp.float32)
     mean_grad = jnp.sum(group_grads, axis=0) / groups
     hess_est = jnp.sum(group_grads * noise_vals, axis=0) / groups / post_std

time: 710 us -> 578 us (0.81)
  other arithmetic: 123 us -> 26.1 us
  local copies, waits for them, and re-layouts: 104 us -> 63.8 us
    unnamed x1 -> x0, other arithmetic: 102 us -> none
    broadcast_in_dim x1 -> x0, local copies, waits for them, and re-layouts: 37.2 us -> none  [local(): gradient[None]]
    another operation x0 -> x2, local copies, waits for them, and re-layouts: none -> 16.2 us  [local(): jnp.stack(jnp.split(gradient[None], lax.axis_size('grp'), axis=1))]
    all_to_all x1 -> x0, local copies, waits for them, and re-layouts: 14.1 us -> none  [local(): lax.all_to_all(gradient[None], 'grp', split_axis=1, concat_axis=0, tiled=...]
    reduce_sum x0 -> x1, other arithmetic: none -> 8.77 us  [local(): hess_est = jnp.sum(group_grads * noise_vals, axis=0) / groups / post_std]
    unnamed x9 -> x39, local copies, waits for them, and re-layouts: 52.4 us -> 47.6 us
where the time goes in v2:
time: 578 us; the launch traced here: 577 us
  waiting for transfers between devices  238 us (41%)
  blocking collectives  207 us (36%)
  local copies, waits for them, and re-layouts  63.8 us (11%)
  other arithmetic  26.1 us (5%)
  matrix products  17.2 us (3%)
  between operations  14.1 us (2%)
  starting transfers between devices  10.4 us (2%)
    all_to_all x1, blocking collectives, local(): lax.all_to_all(jnp.stack(jnp.split(gradient[None], lax.axis_size('grp'),...  207 us
    all_to_all x1, waiting for transfers between devices, local(): lax.all_to_all(samples, 'grp', split_axis=0, concat_axis=1, tiled=True)[0]  130 us
    all_gather x1, waiting for transfers between devices, local(): group_x = lax.all_gather(tokens, 'shard', axis=0, tiled=True)  108 us
    unnamed x39, local copies, waits for them, and re-layouts  47.6 us
    dot_general x1, matrix products, contract_rows(): lax.dot_general(left, right, (((0,), (0,)), ((), ())), preferred_element_...  17.2 us
    another operation x2, local copies, waits for them, and re-layouts, local(): jnp.stack(jnp.split(gradient[None], lax.axis_size('grp'), axis=1))  16.2 us
  transfers between devices with their start and end apart: 2, of which 2 were waited for; matrix products, arithmetic and copies ran while one was open for 0% of the time, Pallas kernels for 0%

profile of v2, /device:TPU:1, one launch (start us, length us, event | category | flops | bytes accessed | tf_op | source)
XLA Modules:
  0.0 576.9 jit_solution(7195888307463575802)
XLA Ops:
  7.2 1.1 multiply_rsqrt_fusion
  8.3 9.4 %fusion.1 = bf16[32,80,1728]{2,1,0:T(8,128)(2,1)} fusion(bf16[32,80,1728]{2,1,0:T(8,128)(2,1)} %param.9, f32[80,1728]{1,0:T(8,128)S(1)} %multiply_rsqrt_fusion, f32[80,1728]{1,0:T(8,128)} %param.7), kind=kLoop, calls=%fused_computation.5 | loop fusion | flops 17694720 | bytes 18800640 | tf_op jit(solution)/shard_map/convert_element_type | solution.py:22
  17.7 0.0 copy-start.3
  17.7 10.2 %all-to-all-start = ((bf16[32,80,1728]{2,1,0:T(8,128)(2,1)}), bf16[32,80,1728]{2,1,0:T(8,128)(2,1)}, u32[]{:S(2)}, u32[]{:S(2)}) async-start(bf16[32,80,1728]{2,1,0:T(8,128)(2,1)} %fusion.1), calls=%async_computation | async-start | bytes 18350080 | tf_op jit(solution)/shard_map/all_to_all | solution.py:26
  27.9 0.2 all-gather.2.cloned.1.call-start
  28.1 0.5 all-gather.2.cloned.1.call-update
  28.6 108.1 %all-gather.2.cloned.1.call-done = bf16[512,2560]{1,0:T(8,128)(2,1)} async-done(((bf16[64,2560]{1,0:T(8,128)(2,1)}), bf16[512,2560]{1,0:T(8,128)(2,1)}) %all-gather.2.cloned.1.call-update) | async-done | bytes 2621456 | tf_op jit(solution)/shard_map/all_gather | solution.py:23
  136.8 129.7 %all-to-all-done = bf16[32,80,1728]{2,1,0:T(8,128)(2,1)} async-done(((bf16[32,80,1728]{2,1,0:T(8,128)(2,1)}), bf16[32,80,1728]{2,1,0:T(8,128)(2,1)}, u32[]{:S(2)}, u32[]{:S(2)}) %all-to-all-start) | async-done | bytes 8847392 | tf_op jit(solution)/shard_map/all_to_all | solution.py:26
  266.4 0.0 copy-done.3
  266.4 17.2 %fusion.3 = bf16[1,2560,1728]{1,2,0:T(8,128)(2,1)} fusion(bf16[512,2560]{1,0:T(8,128)(2,1)} %all-gather.2.cloned.1.call-done, bf16[512,1728]{0,1:T(8,128)(2,1)S(1)} %copy-done.3, bf16[2560,1728]{1,0:T(8,128)(2,1)} %bitcast), kind=kOutput, calls=%fused_computation.8 | convolution fusion | flops 9066774528 | bytes 22085632 | tf_op jit(solution)/shard_map/dot_general | solution.py:13
  283.6 0.0 copy-start
  283.6 2.0 fusion.38
  285.6 2.8 fusion.37
  288.4 2.0 fusion.36
  290.4 2.1 fusion.35
  292.5 2.1 fusion.34
  294.6 2.0 fusion.33
  296.6 2.1 fusion.32
  298.8 2.0 fusion.31
  300.7 1.8 fusion.30
  302.5 2.1 fusion.29
  304.6 2.0 fusion.28
  306.6 2.1 fusion.27
  308.7 2.2 fusion.26
  310.9 2.0 fusion.25
  312.9 2.1 fusion.24
  315.0 2.0 fusion.23
  317.0 0.0 copy-done
  317.0 0.8 fusion.22
  317.8 0.9 fusion.21
  318.7 1.0 fusion.20
  319.7 1.0 fusion.19
  320.7 1.0 fusion.18
  321.7 1.0 fusion.17
  322.7 1.0 fusion.16
  323.7 1.0 fusion.15
  324.6 0.9 fusion.14
  325.5 1.0 fusion.13
  326.5 1.0 fusion.12
  327.4 0.9 fusion.11
  328.3 1.0 fusion.10
  329.3 1.0 fusion.9
  330.3 1.0 fusion.8
  331.3 0.9 fusion.7
  332.2 15.3 %copy.26 = bf16[32,1,80,1728]{3,2,1,0:T(8,128)(2,1)} copy(bf16[32,1,80,1728]{2,3,1,0:T(8,128)(2,1)} %fusion.7) | data formatting | bytes 17694720 | tf_op jit(solution)/shard_map/stack | solution.py:33
  347.5 207.0 %all_to_all.14 = bf16[32,1,80,1728]{3,2,1,0:T(8,128)(2,1)} all-to-all(bf16[32,1,80,1728]{3,2,1,0:T(8,128)(2,1)} %copy.26), channel_id=1, replica_groups=mesh['grp'=32,'shard'=8] {'grp'}, dimensions={0} | all-to-all | bytes 17694720 | tf_op jit(solution)/shard_map/all_to_all | solution.py:32
  554.5 0.0 copy-start.1
  554.5 0.0 copy-start.2
  554.5 8.8 %fusion.2 = f32[80,1728]{1,0:T(8,128)S(1)} fusion(bf16[32,80,1728]{2,1,0:T(8,128)(2,1)} %param.9, bf16[32,1,80,1728]{3,2,1,0:T(8,128)(2,1)} %all_to_all.14), kind=kLoop, calls=%fused_computation.6 | loop fusion | flops 17556480 | bytes 18247680 | tf_op jit(solution)/shard_map/reduce_sum | solution.py:39
  563.3 5.3 convert_reduce_fusion
  568.6 0.0 copy-done.1
  568.6 0.0 copy-done.2
  568.6 1.4 divide_subtract_fusion
Async XLA Ops:
  17.7 248.8 %copy-start.3 = (bf16[512,1728]{0,1:T(8,128)(2,1)S(1)}, bf16[512,1728]{0,1:T(8,128)(2,1)}, u32[]{:S(2)}) copy-start(bf16[512,1728]{0,1:T(8,128)(2,1)} %param.6) | copy-start | bytes 5308420
  17.7 248.8 %all-to-all-start = ((bf16[32,80,1728]{2,1,0:T(8,128)(2,1)}), bf16[32,80,1728]{2,1,0:T(8,128)(2,1)}, u32[]{:S(2)}, u32[]{:S(2)}) async-start(bf16[32,80,1728]{2,1,0:T(8,128)(2,1)} %fusion.1), calls=%async_computation | async-start | bytes 18350080 | tf_op jit(solution)/shard_map/all_to_all | solution.py:26
  27.9 108.9 %all-gather.2.cloned.1.call-start = ((), (), s32[]{:S(2)}) async-start(), calls=%async_computation.2 | async-start | bytes 2949120 | tf_op jit(solution)/shard_map/all_gather | solution.py:23
  283.6 33.3 %copy-start = (bf16[1,2560,1728]{1,2,0:T(8,128)(2,1)S(1)}, bf16[1,2560,1728]{1,2,0:T(8,128)(2,1)}, u32[]{:S(2)}) copy-start(bf16[1,2560,1728]{1,2,0:T(8,128)(2,1)} %fusion.3) | copy-start | bytes 26542084
  554.5 14.1 %copy-start.1 = (f32[80,1728]{1,0:T(8,128)S(1)}, f32[80,1728]{1,0:T(8,128)}, u32[]{:S(2)}) copy-start(f32[80,1728]{1,0:T(8,128)} %param.7) | copy-start | bytes 1658884
  554.5 14.1 %copy-start.2 = (f32[80,1728]{1,0:T(8,128)S(1)}, f32[80,1728]{1,0:T(8,128)}, u32[]{:S(2)}) copy-start(f32[80,1728]{1,0:T(8,128)} %param.8) | copy-start | bytes 1658884
Sparse Core Ops, SparseCore 0:
  31.3 105.4 all-gather.1
